TPU v7x, 256 devices: a whole 4x4x8 slice. The times are simulated.
256 devices in a mesh: req: 16 (over z, core), mp: 16 (over x, y).
Axes of the slice: x: 4, y: 4, z: 8, core: 2. Of those that a mesh axis runs over, the one named last changes fastest.
Arguments:
- tokens: bfloat16 [1568, 7168], P('req', 'mp'), may hold values from -6 to 6
- layernorm_scale: float32 [7168], replicated, may hold values from 0.5 to 1.5
- layernorm_bias: float32 [7168], replicated, may hold values from -3 to 3
- query_key_value_weight: bfloat16 [3, 7168, 6144], P(None, 'req', 'mp'), may hold values from -0.0625 to 0.0625
- query_key_value_bias: float32 [3, 6144], P(None, 'mp'), may hold values from -3 to 3
- adapter_down_weight: bfloat16 [64, 7168, 32], P('req', 'mp'), may hold values from -0.0625 to 0.0625
- adapter_up_weight: bfloat16 [64, 2, 16, 6144], P('req', None, None, 'mp'), may hold values from -1.5 to 1.5
- adapter_index_table: int32 [16, 5], P('req'), may hold values from 0 to 63
- prompt_length_list: int32 [48], P('req'), may hold values from 1 to 32, 960 in all
- cache: bfloat16 [32, 2048, 2, 6144], P('req', None, None, 'mp'), may hold values from -320 to 320, as said below
- cache_length_list: int32 [32], P('req'), may hold values from 1 to 2048, 20480 in all
- output_weight: bfloat16 [6144, 7168], P('mp', 'req'), may hold values from -0.078125 to 0.078125
- output_bias: float32 [7168], P('mp'), may hold values from -3 to 3
Outputs:
- layer_out: bfloat16 [1568, 7168], P('req', 'mp')
Inputs may be any that keep to these rules, and one draw needn't show every extreme that they name: Each prompt fills the first prompt_length_list rows of its slot of 32 rows. Live cache positions are the first cache_length_list of each slot. `cache`: entries mostly of order one, though rare keys may be larger.
All inputs are finite; a program needn't handle non-finite values. No bound on the sum of `prompt_length_list` or of `cache_length_list` on one device may be relied on, other than what follows from the above.
Results may differ from a plain program's by a relative error of at most 0.015.
Values may be sent and summed in bfloat16 or wider, within the bound.
A program may use at most 128 MiB of HBM per device.

v0:
```python
import jax
import jax.numpy as jnp
from jax import lax
from jax.sharding import PartitionSpec as P

HEAD_DIM = 128
ADAPTER_RANK = 16


def layer_norm(row_data, gain_vec, shift_vec):
    values = row_data.astype(jnp.float32)
    average = jnp.mean(values, axis=-1, keepdims=True)
    centred = values - average
    variance = jnp.mean(centred * centred, axis=-1, keepdims=True)
    scaled = centred * lax.rsqrt(variance + 1e-05)
    return (scaled * gain_vec + shift_vec).astype(jnp.bfloat16)


def on_device(
    tokens,
    layernorm_scale,
    layernorm_bias,
    query_key_value_weight,
    query_key_value_bias,
    adapter_down_weight,
    adapter_up_weight,
    adapter_index_table,
    prompt_length_list,
    cache,
    cache_length_list,
    output_weight,
    output_bias,
):
    rows_dev = tokens.shape[0]
    part_cols = tokens.shape[1]
    decode_count = cache.shape[0]
    slot_count = prompt_length_list.shape[0]
    prompt_rows = rows_dev - decode_count
    slot_len = prompt_rows // slot_count
    rank_size = ADAPTER_RANK
    head_count = query_key_value_weight.shape[2] // HEAD_DIM
    score_scale = HEAD_DIM ** (-0.5)
    gathered = lax.all_gather(tokens, "mp", axis=1, tiled=True)
    normed = layer_norm(gathered, layernorm_scale, layernorm_bias)
    column = lax.axis_index("mp")
    slice_m = lax.dynamic_slice_in_dim(normed, column * part_cols, part_cols, 1)
    spread = lax.all_to_all(normed, "req", split_axis=1, concat_axis=0, tiled=True)
    projected = lax.psum_scatter(
        jnp.einsum(
            "rd,cde->rce", spread, query_key_value_weight, preferred_element_type=jnp.float32
        ),
        "req",
        scatter_dimension=0,
        tiled=True,
    )
    projected = projected + query_key_value_bias[None]
    positions = jnp.arange(rows_dev)
    request_slot = jnp.where(
        positions < prompt_rows, positions // slot_len, slot_count + positions - prompt_rows
    )
    slot_match = request_slot[:, None] == jnp.arange(slot_count + decode_count)[None, :]
    row_adapter = jnp.sum(jnp.where(slot_match, adapter_index_table[0][None, :], 0), axis=1)
    adapter_on_device = adapter_down_weight.shape[0]
    owners = lax.axis_size("req")
    owner_row = row_adapter // adapter_on_device
    to_owner = owner_row[None, :] == jnp.arange(owners)[:, None]
    outgoing = jnp.where(to_owner[:, :, None], slice_m[None], jnp.zeros((), jnp.bfloat16))
    labels = jnp.where(to_owner, (row_adapter - owner_row * adapter_on_device)[None, :], -1)
    received_rows = lax.all_to_all(outgoing, "req", split_axis=0, concat_axis=0, tiled=True)
    arrived_labels = lax.all_to_all(labels, "req", split_axis=0, concat_axis=0, tiled=True)
    sources, items = arrived_labels.shape
    selection_mask = (
        arrived_labels[:, :, None] == jnp.arange(adapter_on_device)[None, None, :]
    ).astype(jnp.float32)
    adapter_wise_sums = jnp.einsum(
        "yju,ouv->yjov", received_rows, adapter_down_weight, preferred_element_type=jnp.float32
    )
    reduced_rank_rows = jnp.einsum("ogf,ogft->ogt", selection_mask, adapter_wise_sums)
    reduced_rank_rows = lax.psum(reduced_rank_rows, "mp").astype(jnp.bfloat16)
    broadcast_rank_rows = selection_mask.astype(jnp.bfloat16)[
        :, :, :, None, None
    ] * reduced_rank_rows.reshape(sources, items, 1, 2, rank_size)
    corrections = jnp.einsum(
        "pqwgd,wgdx->pqgx",
        broadcast_rank_rows,
        adapter_up_weight,
        preferred_element_type=jnp.float32,
    ).astype(jnp.bfloat16)
    returned = lax.all_to_all(corrections, "req", split_axis=0, concat_axis=0, tiled=True)
    adapter_delta = jnp.sum(returned.astype(jnp.float32), axis=0)
    queries = (projected[:, 0] + adapter_delta[:, 0]).astype(jnp.bfloat16)
    keys_new = projected[:, 1].astype(jnp.bfloat16)
    values_new = (projected[:, 2] + adapter_delta[:, 1]).astype(jnp.bfloat16)
    prompt_q = queries[:prompt_rows].reshape(slot_count, slot_len, head_count, HEAD_DIM)
    prompt_k = keys_new[:prompt_rows].reshape(slot_count, slot_len, head_count, HEAD_DIM)
    prompt_v = values_new[:prompt_rows].reshape(slot_count, slot_len, head_count, HEAD_DIM)
    scores = (
        jnp.einsum("sihd,sjhd->shij", prompt_q, prompt_k, preferred_element_type=jnp.float32)
        * score_scale
    )
    causal = jnp.arange(slot_len)[None, :] <= jnp.arange(slot_len)[:, None]
    scores = jnp.where(causal[None, None], scores, -1e30)
    highest = jnp.max(scores, axis=3, keepdims=True)
    weights = jnp.where(causal[None, None], jnp.exp(scores - highest), 0.0)
    weights = (weights / jnp.sum(weights, axis=3, keepdims=True)).astype(jnp.bfloat16)
    prompt_out = jnp.einsum(
        "shij,sjhd->sihd", weights, prompt_v, preferred_element_type=jnp.float32
    )
    active = jnp.arange(slot_len)[None, :] < prompt_length_list[:, None]
    prompt_out = (
        jnp.where(active[:, :, None, None], prompt_out, 0.0)
        .astype(jnp.bfloat16)
        .reshape(prompt_rows, -1)
    )
    cache_len = cache.shape[1]
    decode_q = queries[prompt_rows:].reshape(decode_count, head_count, HEAD_DIM)
    decode_k = keys_new[prompt_rows:].reshape(decode_count, head_count, HEAD_DIM)
    decode_v = values_new[prompt_rows:].reshape(decode_count, head_count, HEAD_DIM)
    keys_old = cache[:, :, 0].reshape(decode_count, cache_len, head_count, HEAD_DIM)
    values_old = cache[:, :, 1].reshape(decode_count, cache_len, head_count, HEAD_DIM)
    cache_scores = (
        jnp.einsum("dhe,dthe->dht", decode_q, keys_old, preferred_element_type=jnp.float32)
        * score_scale
    )
    live_cache = jnp.arange(cache_len)[None, None, :] < cache_length_list[:, None, None]
    cache_scores = jnp.where(live_cache, cache_scores, -1e30)
    self_score = (
        jnp.einsum("dhe,dhe->dh", decode_q, decode_k, preferred_element_type=jnp.float32)
        * score_scale
    )
    row_top = jnp.maximum(jnp.max(cache_scores, axis=2), self_score)
    cache_weights = jnp.where(live_cache, jnp.exp(cache_scores - row_top[:, :, None]), 0.0)
    self_weight = jnp.exp(self_score - row_top)
    totals = jnp.sum(cache_weights, axis=2) + self_weight
    cache_weights = (cache_weights / totals[:, :, None]).astype(jnp.bfloat16)
    self_weight = (self_weight / totals).astype(jnp.bfloat16)
    decode_out = jnp.einsum(
        "dht,dthe->dhe", cache_weights, values_old, preferred_element_type=jnp.float32
    )
    decode_out = decode_out + self_weight.astype(jnp.float32)[:, :, None] * decode_v.astype(
        jnp.float32
    )
    decode_out = decode_out.astype(jnp.bfloat16).reshape(decode_count, -1)
    attended = jnp.concatenate([prompt_out, decode_out], axis=0)
    mixed = jnp.dot(
        attended,
        lax.all_gather(output_weight, "req", axis=1, tiled=True),
        preferred_element_type=jnp.float32,
    )
    summed = lax.psum_scatter(
        mixed.astype(jnp.bfloat16), "mp", scatter_dimension=1, tiled=True
    ).astype(jnp.float32)
    return (tokens.astype(jnp.float32) + summed + output_bias[None]).astype(jnp.bfloat16)


def solution(mesh):
    placed = (
        P("req", "mp"),
        P(),
        P(),
        P(None, "req", "mp"),
        P(None, "mp"),
        P("req", "mp", None),
        P("req", None, None, "mp"),
        P("req", None),
        P("req"),
        P("req", None, None, "mp"),
        P("req"),
        P("mp", "req"),
        P("mp"),
    )
    return jax.shard_map(
        on_device, mesh=mesh, in_specs=placed, out_specs=P("req", "mp"), check_vma=False
    )
```

profile of v0, /device:TPU:32, one launch (start us, length us, event | category | flops | bytes accessed | tf_op | source)
XLA Modules:
  0.0 485.0 jit_solution(15356733694840684768)
XLA Ops:
  7.3 54.4 %all-gather.6.cloned.1.call-done = bf16[16,448,98]{1,2,0:T(8,128)(2,1)} async-done(((bf16[1,448,98]{1,2,0:T(8,128)(2,1)}), bf16[16,448,98]{1,2,0:T(8,128)(2,1)}) %all-gather.6.cloned.1.call-update) | async-done | bytes 1404944 | tf_op jit(solution)/shard_map/all_gather | solution.py:43
  61.7 3.6 copy.59
  65.3 4.7 reshape.248
  70.4 2.5 multiply_reduce_fusion
  72.9 1.7 fusion.1
  74.6 3.2 all_to_all.24
  78.7 48.4 %all_to_all.35 = bf16[98,16,448]{2,0,1:T(8,128)(2,1)S(1)} all-to-all(bf16[98,16,448]{2,0,1:T(8,128)(2,1)S(1)} %copy.60), channel_id=1, replica_groups=mesh['req'=16,'mp'=16] {'req'}, dimensions={1} | all-to-all | bytes 2809856 | tf_op jit(solution)/shard_map/all_to_all | solution.py:47
  127.1 1.7 all_to_all.27
  128.8 6.6 %fusion.5 = f32[1568,3,384]{2,0,1:T(8,128)} fusion(bf16[3,448,384]{2,1,0:T(8,128)(2,1)S(1)} %copy-done, bf16[1568,448]{1,0:T(8,128)(2,1)} %all_to_all.27), kind=kOutput, calls=%fused_computation.11 | convolution fusion | flops 1618477056 | bytes 9662464 | tf_op jit(solution)/shard_map/rd,cde->rce/dot_general | solution.py:49
  136.8 4.7 all-to-all-start.1
  141.5 1.0 constant_dynamic-slice_fusion.1
  142.5 1.5 broadcast_select_fusion
  144.0 3.6 all-to-all-done.1
  147.7 5.0 %all-to-all-start.2 = ((bf16[16,98,448]{2,1,0:T(8,128)(2,1)}), bf16[16,98,448]{2,1,0:T(8,128)(2,1)S(1)}, u32[]{:S(2)}, u32[]{:S(2)}) async-start(bf16[16,98,448]{2,1,0:T(8,128)(2,1)} %broadcast_select_fusion), calls=%async_computation.2 | async-start | bytes 3407872 | tf_op jit(solution)/shard_map/all_to_all | solution.py:69
  153.5 46.5 %all-to-all-done.2 = bf16[16,98,448]{2,1,0:T(8,128)(2,1)S(1)} async-done(((bf16[16,98,448]{2,1,0:T(8,128)(2,1)}), bf16[16,98,448]{2,1,0:T(8,128)(2,1)S(1)}, u32[]{:S(2)}, u32[]{:S(2)}) %all-to-all-start.2) | async-done | bytes 1404960 | tf_op jit(solution)/shard_map/all_to_all | solution.py:69
  200.7 74.7 %all-reduce.5 = bf16[16,98,32]{1,2,0:T(8,128)(2,1)S(1)} all-reduce(f32[16,98,32]{1,2,0:T(8,128)S(1)} %fusion.10), channel_id=1, replica_groups=mesh['req'=16,'mp'=16] {'mp'}, use_global_device_ids=true, to_apply=%region_4.5 | all-reduce | flops 50176 | bytes 301056 | tf_op jit(solution)/shard_map/psum | solution.py:79
  276.3 4.0 copy.65
  280.3 7.5 %all-to-all-start.3 = ((bf16[16,98,2,384]{3,2,1,0:T(2,128)(2,1)}), bf16[16,98,2,384]{3,2,1,0:T(2,128)(2,1)S(1)}, u32[]{:S(2)}, u32[]{:S(2)}) async-start(bf16[16,98,2,384]{3,2,1,0:T(2,128)(2,1)} %copy.65), calls=%async_computation.3 | async-start | bytes 4816896 | tf_op jit(solution)/shard_map/all_to_all | solution.py:89
  287.8 13.8 %fusion.54 = (bf16[2,2048,1,384]{3,2,1,0:T(2,128)(2,1)}, bf16[2,2048,1,384]{3,2,1,0:T(2,128)(2,1)}) fusion(bf16[2,2048,2,384]{3,2,1,0:T(2,128)(2,1)} %param.22), kind=kLoop, calls=%fused_computation.103 | loop fusion | bytes 12582912 | tf_op jit(solution)/shard_map/slice | solution.py:119
  301.6 15.3 %copy.100 = bf16[2,2048,1,384]{1,3,0,2:T(8,128)(2,1)} copy(bf16[2,2048,1,384]{3,2,1,0:T(2,128)(2,1)} %get-tuple-element.9) | data formatting | bytes 6291456
  316.9 15.4 %copy.101 = bf16[2,2048,1,384]{1,3,0,2:T(8,128)(2,1)} copy(bf16[2,2048,1,384]{3,2,1,0:T(2,128)(2,1)} %get-tuple-element.10) | data formatting | bytes 6291456
  333.8 1.1 constant_dynamic-slice_fusion
  334.9 1.1 fusion.52
  336.5 8.8 %all-to-all-done.3 = bf16[16,98,2,384]{3,2,1,0:T(2,128)(2,1)S(1)} async-done(((bf16[16,98,2,384]{3,2,1,0:T(2,128)(2,1)}), bf16[16,98,2,384]{3,2,1,0:T(2,128)(2,1)S(1)}, u32[]{:S(2)}, u32[]{:S(2)}) %all-to-all-start.3) | async-done | bytes 2408480 | tf_op jit(solution)/shard_map/all_to_all | solution.py:89
  345.3 2.0 convert_reduce_fusion
  349.3 2.4 fusion.43
  352.3 2.8 fusion.34
  355.2 36.3 %all-gather.4.cloned.1.call-done = bf16[384,7168]{0,1:T(8,128)(2,1)} async-done(((bf16[384,448]{0,1:T(8,128)(2,1)}), bf16[384,7168]{0,1:T(8,128)(2,1)}) %all-gather.4.cloned.1.call-update) | async-done | bytes 5505040 | tf_op jit(solution)/shard_map/all_gather | solution.py:147
  391.5 5.0 %convolution_convert_fusion = bf16[98,7168]{1,0:T(8,128)(2,1)S(1)} fusion(bf16[384,7168]{0,1:T(8,128)(2,1)} %all-gather.4.cloned.1.call-done, bf16[2,384]{1,0:T(2,128)(2,1)S(1)} %bitcast.94, bf16[96,384]{1,0:T(8,128)(2,1)S(1)} %bitcast.91), kind=kOutput, calls=%fused_computation.1 | convolution fusion | flops 540345344 | bytes 6985216 | tf_op jit(solution)/shard_map/dot_general | solution.py:145
  396.5 2.4 copy.98
  398.9 77.8 %reduce-scatter.5.cloned.1.call-done = bf16[448,98]{1,0:T(8,128)(2,1)} async-done(((bf16[7168,98]{1,0:T(8,128)(2,1)}), bf16[448,98]{1,0:T(8,128)(2,1)}) %reduce-scatter.5.cloned.1.call-update) | async-done | bytes 87824
  476.8 1.0 copy.99
  (85 shorter events, 10.4 us)
Async XLA Ops:
  6.5 122.3 %copy-start = (bf16[3,448,384]{2,1,0:T(8,128)(2,1)S(1)}, bf16[3,448,384]{2,1,0:T(8,128)(2,1)}, u32[]{:S(2)}) copy-start(bf16[3,448,384]{2,1,0:T(8,128)(2,1)} %param.16) | copy-start | bytes 3096580
  6.5 55.1 %all-gather.6.cloned.1.call-start = ((), (), s32[]{:S(2)}) async-start(), calls=%async_computation.6 | async-start | bytes 1810432 | tf_op jit(solution)/shard_map/all_gather | solution.py:43
  7.3 326.6 %all-reduce.4.cloned.1.call-start = ((), (), s32[]{:S(2)}) async-start(), calls=%async_computation.8 | async-start | bytes 14450688
  65.3 4.7 copy-start.3
  70.0 2.9 copy-start.2
  70.0 2.9 copy-start.7
  70.0 2.9 copy-start.8
  135.5 0.7 copy-start.13
  135.5 64.4 %copy-start.12 = (bf16[4,448,32]{1,2,0:T(8,128)(2,1)S(1)}, bf16[4,448,32]{1,2,0:T(8,128)(2,1)}, u32[]{:S(2)}) copy-start(bf16[4,448,32]{1,2,0:T(8,128)(2,1)} %param.18) | copy-start | bytes 344068
  136.8 10.8 %all-to-all-start.1 = ((s32[16,1,98]{2,1,0:T(1,128)}), s32[16,1,98]{2,1,0:T(1,128)S(1)}, u32[]{:S(2)}, u32[]{:S(2)}) async-start(s32[16,1,98]{2,1,0:T(1,128)} %compare_select_fusion), calls=%async_computation.1 | async-start | bytes 16384 | tf_op jit(solution)/shard_map/all_to_all | solution.py:70
  144.0 131.3 %copy-start.6 = (bf16[4,2,16,384]{3,2,1,0:T(8,128)(2,1)S(1)}, bf16[4,2,16,384]{3,2,1,0:T(8,128)(2,1)}, u32[]{:S(2)}) copy-start(bf16[4,2,16,384]{3,2,1,0:T(8,128)(2,1)} %param.19) | copy-start | bytes 294916
  147.7 52.2 %all-to-all-start.2 = ((bf16[16,98,448]{2,1,0:T(8,128)(2,1)}), bf16[16,98,448]{2,1,0:T(8,128)(2,1)S(1)}, u32[]{:S(2)}, u32[]{:S(2)}) async-start(bf16[16,98,448]{2,1,0:T(8,128)(2,1)} %broadcast_select_fusion), calls=%async_computation.2 | async-start | bytes 3407872 | tf_op jit(solution)/shard_map/all_to_all | solution.py:69
  152.7 238.8 %all-gather.4.cloned.1.call-start = ((), (), s32[]{:S(2)}) async-start(), calls=%async_computation.5 | async-start | bytes 5849088 | tf_op jit(solution)/shard_map/all_gather | solution.py:147
  280.3 65.1 %all-to-all-start.3 = ((bf16[16,98,2,384]{3,2,1,0:T(2,128)(2,1)}), bf16[16,98,2,384]{3,2,1,0:T(2,128)(2,1)S(1)}, u32[]{:S(2)}, u32[]{:S(2)}) async-start(bf16[16,98,2,384]{3,2,1,0:T(2,128)(2,1)} %copy.65), calls=%async_computation.3 | async-start | bytes 4816896 | tf_op jit(solution)/shard_map/all_to_all | solution.py:89
  287.8 189.0 %reduce-scatter.5.cloned.1.call-start = ((), (), s32[]{:S(2)}) async-start(), calls=%async_computation.7 | async-start | bytes 1949696
  316.9 15.4 %copy-start.15 = (u32[256]{0:T(256)S(1)}, u32[256]{0:T(256)}, u32[]{:S(2)}) copy-start(u32[256]{0:T(256)} %constant.76) | copy-start | bytes 3076
  316.9 16.7 %copy-start.14 = (s32[3]{0:T(128)S(1)}, s32[3]{0:T(128)}, u32[]{:S(2)}) copy-start(s32[3]{0:T(128)} %param.21) | copy-start | bytes 40
  316.9 16.8 %copy-start.11 = (s32[2]{0:T(128)S(1)}, s32[2]{0:T(128)}, u32[]{:S(2)}) copy-start(s32[2]{0:T(128)} %param.23) | copy-start | bytes 28
  316.9 18.0 %copy-start.9 = (f32[3,384]{1,0:T(4,128)S(1)}, f32[3,384]{1,0:T(4,128)}, u32[]{:S(2)}) copy-start(f32[3,384]{1,0:T(4,128)} %param.17) | copy-start | bytes 13828
  336.0 11.4 %copy-start.4 = (f32[98,3,384]{2,1,0:T(4,128)S(1)}, f32[98,3,384]{2,1,0:T(4,128)}, u32[]{:S(2)}) copy-start(f32[98,3,384]{2,1,0:T(4,128)} %get-tuple-element.14) | copy-start | bytes 1354756
  391.5 87.0 %copy-start.1 = (bf16[3,448,384]{2,1,0:T(8,128)(2,1)S(1)}, bf16[3,448,384]{2,1,0:T(8,128)(2,1)}, u32[]{:S(2)}) copy-start(bf16[3,448,384]{2,1,0:T(8,128)(2,1)} %param.16) | copy-start | bytes 3096580
  396.5 81.3 %copy-start.5 = (bf16[98,448]{1,0:T(8,128)(2,1)S(1)}, bf16[98,448]{1,0:T(8,128)(2,1)}, u32[]{:S(2)}) copy-start(bf16[98,448]{1,0:T(8,128)(2,1)} %param.13) | copy-start | bytes 263428
  396.5 81.3 %copy-start.10 = (f32[448]{0:T(512)S(1)}, f32[448]{0:T(512)}, u32[]{:S(2)}) copy-start(f32[448]{0:T(512)} %param.25) | copy-start | bytes 5380
Sparse Core Ops, SparseCore 0:
  9.8 51.8 all-gather.5
  135.6 178.3 all-reduce.3
  315.9 75.5 all-gather.3
  399.1 77.6 reduce-scatter.4
where the time goes:
time: 486 us; the launch traced here: 485 us
  waiting for transfers between devices  229 us (47%)
  blocking collectives  123 us (25%)
  local copies, waits for them, and re-layouts  71 us (15%)
  matrix products  18.9 us (4%)
  starting transfers between devices  17.3 us (4%)
  between operations  14.1 us (3%)
  other arithmetic  11.7 us (2%)
    unnamed x6, waiting for transfers between devices  79.3 us
    psum x1, blocking collectives, on_device(): reduced_rank_rows = lax.psum(reduced_rank_rows, 'mp').astype(jnp.bfloat16)  74.7 us
    all_gather x1, waiting for transfers between devices, on_device(): gathered = lax.all_gather(tokens, 'mp', axis=1, tiled=True)  54.4 us
    all_to_all x1, blocking collectives, on_device(): lax.all_to_all(normed, 'req', split_axis=1, concat_axis=0, tiled=True)  48.4 us
    all_to_all x1, waiting for transfers between devices, on_device(): lax.all_to_all(outgoing, 'req', split_axis=0, concat_axis=0, tiled=True)  46.5 us
    unnamed x40, local copies, waits for them, and re-layouts  36.5 us
    all_gather x1, waiting for transfers between devices, on_device(): lax.all_gather(output_weight, 'req', axis=1, tiled=True)  36.3 us
    slice x1, local copies, waits for them, and re-layouts, on_device(): cache[:, :, 0].reshape(decode_count, cache_len, head_count, HEAD_DIM)  13.8 us
  transfers between devices with their start and end apart: 7, of which 6 were waited for; matrix products, arithmetic and copies ran while one was open for 14% of the time, Pallas kernels for 0%

commit v1 on v0

--- a/solution.py
+++ b/solution.py
@@ -5,6 +5,22 @@
 
 HEAD_DIM = 128
 ADAPTER_RANK = 16
+
+
+def collect(x, axis, dim):
+    ways, here, step = (lax.axis_size(axis), lax.axis_index(axis), x.shape[dim])
+    shape = [n * ways if d == dim else n for d, n in enumerate(x.shape)]
+    full = lax.dynamic_update_slice_in_dim(jnp.zeros(shape, x.dtype), x, here * step, axis=dim)
+    going_up = going_down = x
+    for far in range(1, ways // 2 + 1):
+        going_up = lax.ppermute(going_up, axis, [(d, (d + 1) % ways) for d in range(ways)])
+        full = lax.dynamic_update_slice_in_dim(full, going_up, (here - far) % ways * step, axis=dim)
+        if 2 * far < ways:
+            going_down = lax.ppermute(going_down, axis, [(d, (d - 1) % ways) for d in range(ways)])
+            full = lax.dynamic_update_slice_in_dim(
+                full, going_down, (here + far) % ways * step, axis=dim
+            )
+    return full
 
 
 def layer_norm(row_data, gain_vec, shift_vec):
@@ -142,11 +158,7 @@
     )
     decode_out = decode_out.astype(jnp.bfloat16).reshape(decode_count, -1)
     attended = jnp.concatenate([prompt_out, decode_out], axis=0)
-    mixed = jnp.dot(
-        attended,
-        lax.all_gather(output_weight, "req", axis=1, tiled=True),
-        preferred_element_type=jnp.float32,
-    )
+    mixed = jnp.dot(attended, collect(output_weight, "req", 1), preferred_element_type=jnp.float32)
     summed = lax.psum_scatter(
         mixed.astype(jnp.bfloat16), "mp", scatter_dimension=1, tiled=True
     ).astype(jnp.float32)

time: 486 us -> 509 us (1.047)
  blocking collectives: 123 us -> 74.5 us
  starting transfers between devices: 17.3 us -> 44.3 us
  local copies, waits for them, and re-layouts: 71 us -> 92.3 us
  waiting for transfers between devices: 229 us -> 249 us
    unnamed x6 -> x5, waiting for transfers between devices: 79.3 us -> 132 us
    all_to_all x1 -> x0, blocking collectives: 48.4 us -> none  [on_device(): lax.all_to_all(normed, 'req', split_axis=1, concat_axis=0, tiled=True)]
    ppermute x0 -> x15, waiting for transfers between devices: none -> 39 us  [the longest x8 39 us: collect(): lax.ppermute(going_up, axis, [(d, (d + 1) % ways) for d in range(ways)])]
    all_gather x1 -> x0, waiting for transfers between devices: 36.3 us -> none  [on_device(): lax.all_gather(output_weight, 'req', axis=1, tiled=True)]
    dynamic_update_slice x0 -> x16, local copies, waits for them, and re-layouts: none -> 15.3 us  [the longest x8 7.15 us: collect(): lax.dynamic_update_slice_in_dim(full, going_up, (here - far) % ways * ste...]
    all_to_all x1, waiting for transfers between devices: 46.5 us -> 33.7 us  [on_device(): lax.all_to_all(outgoing, 'req', split_axis=0, concat_axis=0, tiled=True)]
    ppermute x0 -> x15, starting transfers between devices: none -> 12.6 us  [the longest x7 12.3 us: collect(): lax.ppermute(going_down, axis, [(d, (d - 1) % ways) for d in range(ways)])]
    all_gather x1, waiting for transfers between devices: 54.4 us -> 44.5 us  [on_device(): gathered = lax.all_gather(tokens, 'mp', axis=1, tiled=True)]
  transfers between devices with their start and end apart: 7 -> 22, of which waited for: 6 -> 11; matrix products, arithmetic and copies ran while one was open for 14% -> 19% of each run, Pallas kernels for 0% -> 0%
where the time goes in v1:
time: 509 us; the launch traced here: 508 us
  waiting for transfers between devices  249 us (49%)
  local copies, waits for them, and re-layouts  92.3 us (18%)
  blocking collectives  74.5 us (15%)
  starting transfers between devices  44.3 us (9%)
  matrix products  20.4 us (4%)
  between operations  14.5 us (3%)
  other arithmetic  12.5 us (2%)
    unnamed x5, waiting for transfers between devices  132 us
    psum x1, blocking collectives, on_device(): reduced_rank_rows = lax.psum(reduced_rank_rows, 'mp').astype(jnp.bfloat16)  74.5 us
    all_gather x1, waiting for transfers between devices, on_device(): gathered = lax.all_gather(tokens, 'mp', axis=1, tiled=True)  44.5 us
    ppermute x8, waiting for transfers between devices, collect(): lax.ppermute(going_up, axis, [(d, (d + 1) % ways) for d in range(ways)])  39 us
    unnamed x40, local copies, waits for them, and re-layouts  38.3 us
    all_to_all x1, waiting for transfers between devices, on_device(): lax.all_to_all(outgoing, 'req', split_axis=0, concat_axis=0, tiled=True)  33.7 us
    slice x1, local copies, waits for them, and re-layouts, on_device(): cache[:, :, 0].reshape(decode_count, cache_len, head_count, HEAD_DIM)  13.8 us
    ppermute x7, starting transfers between devices, collect(): lax.ppermute(going_down, axis, [(d, (d - 1) % ways) for d in range(ways)])  12.3 us
  transfers between devices with their start and end apart: 22, of which 11 were waited for; matrix products, arithmetic and copies ran while one was open for 19% of the time, Pallas kernels for 0%

profile of v1, /device:TPU:32, one launch (start us, length us, event | category | flops | bytes accessed | tf_op | source)
XLA Modules:
  0.0 507.8 jit_solution(14164889770790790078)
XLA Ops:
  8.6 8.6 %all-to-all-start.1 = ((s32[16,1,98]{2,1,0:T(1,128)}), s32[16,1,98]{2,1,0:T(1,128)S(1)}, u32[]{:S(2)}, u32[]{:S(2)}) async-start(s32[16,1,98]{2,1,0:T(1,128)} %compare_select_fusion), calls=%async_computation.1 | async-start | bytes 16384 | tf_op jit(solution)/shard_map/all_to_all | solution.py:86
  17.2 44.5 %all-gather.3.cloned.1.call-done = bf16[16,448,98]{1,2,0:T(8,128)(2,1)} async-done(((bf16[1,448,98]{1,2,0:T(8,128)(2,1)}), bf16[16,448,98]{1,2,0:T(8,128)(2,1)}) %all-gather.3.cloned.1.call-update) | async-done | bytes 1404944 | tf_op jit(solution)/shard_map/all_gather | solution.py:59
  61.7 3.8 copy.59
  65.5 4.6 reshape.248
  70.4 2.5 multiply_reduce_fusion
  76.2 7.5 %all-to-all-start.2 = ((bf16[16,98,448]{2,1,0:T(8,128)(2,1)}), bf16[16,98,448]{2,1,0:T(8,128)(2,1)}, u32[]{:S(2)}, u32[]{:S(2)}) async-start(bf16[16,98,448]{2,1,0:T(8,128)(2,1)} %broadcast_select_fusion), calls=%async_computation.2 | async-start | bytes 3407872 | tf_op jit(solution)/shard_map/all_to_all | solution.py:85
  83.7 3.2 all_to_all.24
  89.1 33.7 %all-to-all-done.2 = bf16[16,98,448]{2,1,0:T(8,128)(2,1)} async-done(((bf16[16,98,448]{2,1,0:T(8,128)(2,1)}), bf16[16,98,448]{2,1,0:T(8,128)(2,1)}, u32[]{:S(2)}, u32[]{:S(2)}) %all-to-all-start.2) | async-done | bytes 1404960 | tf_op jit(solution)/shard_map/all_to_all | solution.py:85
  122.7 6.6 %all-to-all-start = ((bf16[98,16,448]{2,0,1:T(8,128)(2,1)}), bf16[98,16,448]{2,0,1:T(8,128)(2,1)S(1)}, u32[]{:S(2)}, u32[]{:S(2)}) async-start(bf16[98,16,448]{2,0,1:T(8,128)(2,1)} %copy.60), calls=%async_computation | async-start | bytes 3407872 | tf_op jit(solution)/shard_map/all_to_all | solution.py:63
  131.1 2.2 fusion.10
  133.4 74.5 %all-reduce.5 = bf16[16,98,32]{1,2,0:T(8,128)(2,1)S(1)} all-reduce(f32[16,98,32]{1,2,0:T(8,128)S(1)} %fusion.10), channel_id=1, replica_groups=mesh['req'=16,'mp'=16] {'mp'}, use_global_device_ids=true, to_apply=%region_4.5 | all-reduce | flops 50176 | bytes 301056 | tf_op jit(solution)/shard_map/psum | solution.py:95
  208.8 3.9 copy.65
  213.9 8.7 %all-to-all-start.3 = ((bf16[16,98,2,384]{3,2,1,0:T(2,128)(2,1)}), bf16[16,98,2,384]{3,2,1,0:T(2,128)(2,1)S(1)}, u32[]{:S(2)}, u32[]{:S(2)}) async-start(bf16[16,98,2,384]{3,2,1,0:T(2,128)(2,1)} %copy.65), calls=%async_computation.3 | async-start | bytes 4816896 | tf_op jit(solution)/shard_map/all_to_all | solution.py:105
  222.6 2.9 all_to_all.27
  225.5 6.6 %fusion.5 = f32[1568,3,384]{2,0,1:T(8,128)} fusion(bf16[3,448,384]{2,1,0:T(8,128)(2,1)S(1)} %copy-done, bf16[1568,448]{1,0:T(8,128)(2,1)} %all_to_all.27), kind=kOutput, calls=%fused_computation.11 | convolution fusion | flops 1618477056 | bytes 9662464 | tf_op jit(solution)/shard_map/rd,cde->rce/dot_general | solution.py:65
  232.4 13.8 %fusion.54 = (bf16[2,2048,1,384]{3,2,1,0:T(2,128)(2,1)}, bf16[2,2048,1,384]{3,2,1,0:T(2,128)(2,1)}) fusion(bf16[2,2048,2,384]{3,2,1,0:T(2,128)(2,1)} %param.22), kind=kLoop, calls=%fused_computation.119 | loop fusion | bytes 12582912 | tf_op jit(solution)/shard_map/slice | solution.py:135
  248.3 15.4 %copy.100 = bf16[2,2048,1,384]{1,3,0,2:T(8,128)(2,1)} copy(bf16[2,2048,1,384]{3,2,1,0:T(2,128)(2,1)} %get-tuple-element.9) | data formatting | bytes 6291456
  263.7 15.4 %copy.101 = bf16[2,2048,1,384]{1,3,0,2:T(8,128)(2,1)} copy(bf16[2,2048,1,384]{3,2,1,0:T(2,128)(2,1)} %get-tuple-element.10) | data formatting | bytes 6291456
  280.4 11.9 %collective-permute-done.2 = bf16[384,448]{0,1:T(8,128)(2,1)S(1)} collective-permute-done((bf16[384,448]{0,1:T(8,128)(2,1)}, bf16[384,448]{0,1:T(8,128)(2,1)S(1)}, u32[]{:S(2)}, u32[]{:S(2)}) %collective-permute-start.2) | collective-permute-done | bytes 344096 | tf_op jit(solution)/shard_map/ppermute | solution.py:16
  294.5 2.8 broadcast_in_dim.145
  299.1 3.5 collective-permute-done.4
  307.9 5.0 collective-permute-done.6
  316.9 6.2 %collective-permute-done.8 = bf16[384,448]{0,1:T(8,128)(2,1)S(1)} collective-permute-done((bf16[384,448]{0,1:T(8,128)(2,1)S(1)}, bf16[384,448]{0,1:T(8,128)(2,1)S(1)}, u32[]{:S(2)}, u32[]{:S(2)}) %collective-permute-start.8) | collective-permute-done | bytes 344096 | tf_op jit(solution)/shard_map/ppermute | solution.py:16
  327.2 5.4 %collective-permute-done.10 = bf16[384,448]{0,1:T(8,128)(2,1)S(1)} collective-permute-done((bf16[384,448]{0,1:T(8,128)(2,1)S(1)}, bf16[384,448]{0,1:T(8,128)(2,1)S(1)}, u32[]{:S(2)}, u32[]{:S(2)}) %collective-permute-start.10) | collective-permute-done | bytes 344096 | tf_op jit(solution)/shard_map/ppermute | solution.py:16
  336.7 2.6 collective-permute-done.12
  341.6 4.4 collective-permute-done.14
  346.7 50.8 %all-reduce.4.cloned.1.call-done = f32[1568,3,384]{2,0,1:T(8,128)} async-done(((f32[1568,3,384]{2,0,1:T(8,128)}), f32[1568,3,384]{2,0,1:T(8,128)}) %all-reduce.4.cloned.1.call-update) | async-done | bytes 7225360
  404.8 2.4 fusion.43
  407.8 2.8 fusion.34
  411.4 5.0 convolution_convert_fusion
  416.4 2.4 copy.98
  418.8 80.8 %reduce-scatter.5.cloned.1.call-done = bf16[448,98]{1,0:T(8,128)(2,1)} async-done(((bf16[7168,98]{1,0:T(8,128)(2,1)}), bf16[448,98]{1,0:T(8,128)(2,1)}) %reduce-scatter.5.cloned.1.call-update) | async-done | bytes 87824
  (130 shorter events, 49.1 us)
Async XLA Ops:
  6.5 218.9 %copy-start = (bf16[3,448,384]{2,1,0:T(8,128)(2,1)S(1)}, bf16[3,448,384]{2,1,0:T(8,128)(2,1)}, u32[]{:S(2)}) copy-start(bf16[3,448,384]{2,1,0:T(8,128)(2,1)} %param.16) | copy-start | bytes 3096580
  6.5 55.1 %all-gather.3.cloned.1.call-start = ((), (), s32[]{:S(2)}) async-start(), calls=%async_computation.5 | async-start | bytes 1810432 | tf_op jit(solution)/shard_map/all_gather | solution.py:59
  8.6 67.6 %all-to-all-start.1 = ((s32[16,1,98]{2,1,0:T(1,128)}), s32[16,1,98]{2,1,0:T(1,128)S(1)}, u32[]{:S(2)}, u32[]{:S(2)}) async-start(s32[16,1,98]{2,1,0:T(1,128)} %compare_select_fusion), calls=%async_computation.1 | async-start | bytes 16384 | tf_op jit(solution)/shard_map/all_to_all | solution.py:86
  76.2 46.5 %all-to-all-start.2 = ((bf16[16,98,448]{2,1,0:T(8,128)(2,1)}), bf16[16,98,448]{2,1,0:T(8,128)(2,1)}, u32[]{:S(2)}, u32[]{:S(2)}) async-start(bf16[16,98,448]{2,1,0:T(8,128)(2,1)} %broadcast_select_fusion), calls=%async_computation.2 | async-start | bytes 3407872 | tf_op jit(solution)/shard_map/all_to_all | solution.py:85
  83.7 47.4 %copy-start.13 = (bf16[4,448,32]{1,2,0:T(8,128)(2,1)S(1)}, bf16[4,448,32]{1,2,0:T(8,128)(2,1)}, u32[]{:S(2)}) copy-start(bf16[4,448,32]{1,2,0:T(8,128)(2,1)} %param.18) | copy-start | bytes 344068
  87.0 120.9 %copy-start.7 = (bf16[4,2,16,384]{3,2,1,0:T(8,128)(2,1)S(1)}, bf16[4,2,16,384]{3,2,1,0:T(8,128)(2,1)}, u32[]{:S(2)}) copy-start(bf16[4,2,16,384]{3,2,1,0:T(8,128)(2,1)} %param.19) | copy-start | bytes 294916
  122.7 89.9 %all-to-all-start = ((bf16[98,16,448]{2,0,1:T(8,128)(2,1)}), bf16[98,16,448]{2,0,1:T(8,128)(2,1)S(1)}, u32[]{:S(2)}, u32[]{:S(2)}) async-start(bf16[98,16,448]{2,0,1:T(8,128)(2,1)} %copy.60), calls=%async_computation | async-start | bytes 3407872 | tf_op jit(solution)/shard_map/all_to_all | solution.py:63
  129.4 116.8 %collective-permute-start = (bf16[384,448]{0,1:T(8,128)(2,1)}, bf16[384,448]{0,1:T(8,128)(2,1)}, u32[]{:S(2)}, u32[]{:S(2)}) collective-permute-start(bf16[384,448]{0,1:T(8,128)(2,1)} %param.24), channel_id=1, source_target_pairs={{0,16},{16,32},{32,48},{48,64},{64,80},{80,96},{96,112},{112,128},... | collective-permute-start | bytes 1032200 | tf_op jit(solution)/shard_map/ppermute | solution.py:16
  129.5 116.8 %collective-permute-start.1 = (bf16[384,448]{0,1:T(8,128)(2,1)}, bf16[384,448]{0,1:T(8,128)(2,1)}, u32[]{:S(2)}, u32[]{:S(2)}) collective-permute-start(bf16[384,448]{0,1:T(8,128)(2,1)} %param.24), channel_id=1, source_target_pairs={{0,240},{16,0},{32,16},{48,32},{64,48},{80,64},{96,80},{112,96},{1... | collective-permute-start | bytes 1032200 | tf_op jit(solution)/shard_map/ppermute | solution.py:19
  213.9 186.3 %all-to-all-start.3 = ((bf16[16,98,2,384]{3,2,1,0:T(2,128)(2,1)}), bf16[16,98,2,384]{3,2,1,0:T(2,128)(2,1)S(1)}, u32[]{:S(2)}, u32[]{:S(2)}) async-start(bf16[16,98,2,384]{3,2,1,0:T(2,128)(2,1)} %copy.65), calls=%async_computation.3 | async-start | bytes 4816896 | tf_op jit(solution)/shard_map/all_to_all | solution.py:105
  222.5 175.0 %all-reduce.4.cloned.1.call-start = ((), (), s32[]{:S(2)}) async-start(), calls=%async_computation.7 | async-start | bytes 14450688
  232.1 15.8 %copy-start.12 = (s32[2]{0:T(128)S(1)}, s32[2]{0:T(128)}, u32[]{:S(2)}) copy-start(s32[2]{0:T(128)} %param.23) | copy-start | bytes 28
  232.2 267.4 %reduce-scatter.5.cloned.1.call-start = ((), (), s32[]{:S(2)}) async-start(), calls=%async_computation.6 | async-start | bytes 1949696
  246.2 46.2 %collective-permute-start.2 = (bf16[384,448]{0,1:T(8,128)(2,1)}, bf16[384,448]{0,1:T(8,128)(2,1)S(1)}, u32[]{:S(2)}, u32[]{:S(2)}) collective-permute-start(bf16[384,448]{0,1:T(8,128)(2,1)} %collective-permute-done), channel_id=1, source_target_pairs={{0,16},{16,32},{32,48},{48,64},{64,80},{80,96},{96,112},{112,128},... | collective-permute-start | bytes 1032200 | tf_op jit(solution)/shard_map/ppermute | solution.py:16
  246.3 46.1 %collective-permute-start.3 = (bf16[384,448]{0,1:T(8,128)(2,1)}, bf16[384,448]{0,1:T(8,128)(2,1)S(1)}, u32[]{:S(2)}, u32[]{:S(2)}) collective-permute-start(bf16[384,448]{0,1:T(8,128)(2,1)} %collective-permute-done.1), channel_id=1, source_target_pairs={{0,240},{16,0},{32,16},{48,32},{64,48},{80,64},{96,80},{112,96},{1... | collective-permute-start | bytes 1032200 | tf_op jit(solution)/shard_map/ppermute | solution.py:19
  263.7 15.4 %copy-start.15 = (u32[256]{0:T(256)S(1)}, u32[256]{0:T(256)}, u32[]{:S(2)}) copy-start(u32[256]{0:T(256)} %constant.172) | copy-start | bytes 3076
  263.7 28.7 %copy-start.14 = (s32[3]{0:T(128)S(1)}, s32[3]{0:T(128)}, u32[]{:S(2)}) copy-start(s32[3]{0:T(128)} %param.21) | copy-start | bytes 40
  292.3 10.3 %collective-permute-start.4 = (bf16[384,448]{0,1:T(8,128)(2,1)S(1)}, bf16[384,448]{0,1:T(8,128)(2,1)S(1)}, u32[]{:S(2)}, u32[]{:S(2)}) collective-permute-start(bf16[384,448]{0,1:T(8,128)(2,1)S(1)} %collective-permute-done.2), channel_id=1, source_target_pairs={{0,16},{16,32},{32,48},{48,64},{64,80},{80,96},{96,112},{112,128},... | collective-permute-start | bytes 1032200 | tf_op jit(solution)/shard_map/ppermute | solution.py:16
  292.4 12.0 %collective-permute-start.5 = (bf16[384,448]{0,1:T(8,128)(2,1)S(1)}, bf16[384,448]{0,1:T(8,128)(2,1)S(1)}, u32[]{:S(2)}, u32[]{:S(2)}) collective-permute-start(bf16[384,448]{0,1:T(8,128)(2,1)S(1)} %collective-permute-done.3), channel_id=1, source_target_pairs={{0,240},{16,0},{32,16},{48,32},{64,48},{80,64},{96,80},{112,96},{1... | collective-permute-start | bytes 1032200 | tf_op jit(solution)/shard_map/ppermute | solution.py:19
  302.6 10.2 %collective-permute-start.6 = (bf16[384,448]{0,1:T(8,128)(2,1)S(1)}, bf16[384,448]{0,1:T(8,128)(2,1)S(1)}, u32[]{:S(2)}, u32[]{:S(2)}) collective-permute-start(bf16[384,448]{0,1:T(8,128)(2,1)S(1)} %collective-permute-done.4), channel_id=1, source_target_pairs={{0,16},{16,32},{32,48},{48,64},{64,80},{80,96},{96,112},{112,128},... | collective-permute-start | bytes 1032200 | tf_op jit(solution)/shard_map/ppermute | solution.py:16
  302.6 96.0 %copy-start.10 = (f32[3,384]{1,0:T(4,128)S(1)}, f32[3,384]{1,0:T(4,128)}, u32[]{:S(2)}) copy-start(f32[3,384]{1,0:T(4,128)} %param.17) | copy-start | bytes 13828
  304.4 10.0 %collective-permute-start.7 = (bf16[384,448]{0,1:T(8,128)(2,1)S(1)}, bf16[384,448]{0,1:T(8,128)(2,1)S(1)}, u32[]{:S(2)}, u32[]{:S(2)}) collective-permute-start(bf16[384,448]{0,1:T(8,128)(2,1)S(1)} %collective-permute-done.5), channel_id=1, source_target_pairs={{0,240},{16,0},{32,16},{48,32},{64,48},{80,64},{96,80},{112,96},{1... | collective-permute-start | bytes 1032200 | tf_op jit(solution)/shard_map/ppermute | solution.py:19
  312.8 10.3 %collective-permute-start.8 = (bf16[384,448]{0,1:T(8,128)(2,1)S(1)}, bf16[384,448]{0,1:T(8,128)(2,1)S(1)}, u32[]{:S(2)}, u32[]{:S(2)}) collective-permute-start(bf16[384,448]{0,1:T(8,128)(2,1)S(1)} %collective-permute-done.6), channel_id=1, source_target_pairs={{0,16},{16,32},{32,48},{48,64},{64,80},{80,96},{96,112},{112,128},... | collective-permute-start | bytes 1032200 | tf_op jit(solution)/shard_map/ppermute | solution.py:16
  314.4 10.3 %collective-permute-start.9 = (bf16[384,448]{0,1:T(8,128)(2,1)S(1)}, bf16[384,448]{0,1:T(8,128)(2,1)S(1)}, u32[]{:S(2)}, u32[]{:S(2)}) collective-permute-start(bf16[384,448]{0,1:T(8,128)(2,1)S(1)} %collective-permute-done.7), channel_id=1, source_target_pairs={{0,240},{16,0},{32,16},{48,32},{64,48},{80,64},{96,80},{112,96},{1... | collective-permute-start | bytes 1032200 | tf_op jit(solution)/shard_map/ppermute | solution.py:19
  323.2 9.5 %collective-permute-start.10 = (bf16[384,448]{0,1:T(8,128)(2,1)S(1)}, bf16[384,448]{0,1:T(8,128)(2,1)S(1)}, u32[]{:S(2)}, u32[]{:S(2)}) collective-permute-start(bf16[384,448]{0,1:T(8,128)(2,1)S(1)} %collective-permute-done.8), channel_id=1, source_target_pairs={{0,16},{16,32},{32,48},{48,64},{64,80},{80,96},{96,112},{112,128},... | collective-permute-start | bytes 1032200 | tf_op jit(solution)/shard_map/ppermute | solution.py:16
  324.7 9.5 %collective-permute-start.11 = (bf16[384,448]{0,1:T(8,128)(2,1)S(1)}, bf16[384,448]{0,1:T(8,128)(2,1)S(1)}, u32[]{:S(2)}, u32[]{:S(2)}) collective-permute-start(bf16[384,448]{0,1:T(8,128)(2,1)S(1)} %collective-permute-done.9), channel_id=1, source_target_pairs={{0,240},{16,0},{32,16},{48,32},{64,48},{80,64},{96,80},{112,96},{1... | collective-permute-start | bytes 1032200 | tf_op jit(solution)/shard_map/ppermute | solution.py:19
  332.6 6.7 %collective-permute-start.12 = (bf16[384,448]{0,1:T(8,128)(2,1)S(1)}, bf16[384,448]{0,1:T(8,128)(2,1)S(1)}, u32[]{:S(2)}, u32[]{:S(2)}) collective-permute-start(bf16[384,448]{0,1:T(8,128)(2,1)S(1)} %collective-permute-done.10), channel_id=1, source_target_pairs={{0,16},{16,32},{32,48},{48,64},{64,80},{80,96},{96,112},{112,128},... | collective-permute-start | bytes 1032200 | tf_op jit(solution)/shard_map/ppermute | solution.py:16
  334.2 6.7 %collective-permute-start.13 = (bf16[384,448]{0,1:T(8,128)(2,1)S(1)}, bf16[384,448]{0,1:T(8,128)(2,1)S(1)}, u32[]{:S(2)}, u32[]{:S(2)}) collective-permute-start(bf16[384,448]{0,1:T(8,128)(2,1)S(1)} %collective-permute-done.11), channel_id=1, source_target_pairs={{0,240},{16,0},{32,16},{48,32},{64,48},{80,64},{96,80},{112,96},{1... | collective-permute-start | bytes 1032200 | tf_op jit(solution)/shard_map/ppermute | solution.py:19
  339.3 6.7 %collective-permute-start.14 = (bf16[384,448]{0,1:T(8,128)(2,1)S(1)}, bf16[384,448]{0,1:T(8,128)(2,1)S(1)}, u32[]{:S(2)}, u32[]{:S(2)}) collective-permute-start(bf16[384,448]{0,1:T(8,128)(2,1)S(1)} %collective-permute-done.12), channel_id=1, source_target_pairs={{0,16},{16,32},{32,48},{48,64},{64,80},{80,96},{96,112},{112,128},... | collective-permute-start | bytes 1032200 | tf_op jit(solution)/shard_map/ppermute | solution.py:16
  411.3 90.0 %copy-start.1 = (bf16[3,448,384]{2,1,0:T(8,128)(2,1)S(1)}, bf16[3,448,384]{2,1,0:T(8,128)(2,1)}, u32[]{:S(2)}) copy-start(bf16[3,448,384]{2,1,0:T(8,128)(2,1)} %param.16) | copy-start | bytes 3096580
  411.4 89.3 %copy-start.6 = (bf16[98,448]{1,0:T(8,128)(2,1)S(1)}, bf16[98,448]{1,0:T(8,128)(2,1)}, u32[]{:S(2)}) copy-start(bf16[98,448]{1,0:T(8,128)(2,1)} %param.13) | copy-start | bytes 263428
  411.4 89.2 %copy-start.11 = (f32[448]{0:T(512)S(1)}, f32[448]{0:T(512)}, u32[]{:S(2)}) copy-start(f32[448]{0:T(512)} %param.25) | copy-start | bytes 5380
  (6 other events, 28.5 us)
Sparse Core Ops, SparseCore 0:
  9.8 51.8 all-gather.2
  232.3 165.2 all-reduce.3
  418.9 80.6 reduce-scatter.4
